TPU v7x, 32 devices: a whole 2x2x4 slice. The times are simulated.
32 devices in a mesh: dp: 16 (over z, x, core), tensor: 2 (over y).
Axes of the slice: x: 2, y: 2, z: 4, core: 2. Of those that a mesh axis runs over, the one named last changes fastest.
Arguments:
- inputs: float32 [16, 256, 768], P('dp'), may hold values from -6 to 6
- condition: float32 [16, 768], P('dp'), may hold values from -2.5 to 2.5
- cotangent: float32 [16, 256, 768], P('dp'), may hold values from -6 to 6
- w_qkv: float32 [2, 768, 3, 768], P(None, None, None, 'tensor'), may hold values from -0.21875 to 0.21875
- b_qv: float32 [2, 2, 768], P(None, None, 'tensor'), may hold values from -1.25 to 1.25
- w_out: float32 [2, 768, 768], P(None, 'tensor'), may hold values from -0.875 to 0.875
- b_out: float32 [2, 768], replicated, may hold values from -3 to 3
- w_up: float32 [2, 768, 3072], P(None, None, 'tensor'), may hold values from -0.21875 to 0.21875
- b_up: float32 [2, 3072], P(None, 'tensor'), may hold values from -3 to 3
- w_down: float32 [2, 3072, 768], P(None, 'tensor'), may hold values from -0.109375 to 0.109375
- b_down: float32 [2, 768], replicated, may hold values from -3 to 3
- w_mod: float32 [2, 768, 4608], P(None, None, 'tensor'), may hold values from -0.21875 to 0.21875
- b_mod: float32 [2, 4608], P(None, 'tensor'), may hold values from -0.75 to 0.75
Outputs:
- outputs: float32 [16, 256, 768], P('dp')
- grad_inputs: float32 [16, 256, 768], P('dp')
- grad_condition: float32 [16, 768], P('dp')
- grad_w_qkv: float32 [2, 768, 3, 768], P(None, 'dp', None, 'tensor')
- grad_b_qv: float32 [2, 2, 768], P(None, None, 'tensor')
- grad_w_out: float32 [2, 768, 768], P(None, 'tensor', 'dp')
- grad_b_out: float32 [2, 768], replicated
- grad_w_up: float32 [2, 768, 3072], P(None, 'dp', 'tensor')
- grad_b_up: float32 [2, 3072], P(None, 'tensor')
- grad_w_down: float32 [2, 3072, 768], P(None, 'tensor', 'dp')
- grad_b_down: float32 [2, 768], replicated
- grad_w_mod: float32 [2, 768, 4608], P(None, 'dp', 'tensor')
- grad_b_mod: float32 [2, 4608], P(None, 'tensor')
All inputs are finite; a program needn't handle non-finite values.
Results may differ from a plain program's by a relative error of at most 0.0003.
Values sent between devices are 32-bit elements; how exact they have to be, the bound alone decides.
A program may use at most 256 MiB of HBM per device.

v0:
```python
import jax
import jax.numpy as jnp
from jax import lax
from jax.sharding import PartitionSpec as P

HEAD_DIM = 64
high = lax.Precision.HIGH
eps_norm = 1e-06


def layer_norm(values):
    row_mean = jnp.mean(values, axis=-1, keepdims=True)
    centred = values - row_mean
    row_var = jnp.mean(centred * centred, axis=-1, keepdims=True)
    return centred * lax.rsqrt(row_var + eps_norm)


def gelu_tanh(values):
    return jax.nn.gelu(values, approximate=True)


def silu_slope(values):
    sigma = jax.nn.sigmoid(values)
    return sigma * (1.0 + values * (1.0 - sigma))


def pair_sum(value):
    if lax.axis_size("tensor") == 2:
        return value + lax.ppermute(value, "tensor", [(0, 1), (1, 0)])
    return lax.psum(value, "tensor")


def pair_gather(value, axis):
    if lax.axis_size("tensor") == 2:
        other = lax.ppermute(value, "tensor", [(0, 1), (1, 0)])
        first = lax.axis_index("tensor") == 0
        low = jnp.where(first, value, other)
        top = jnp.where(first, other, value)
        return jnp.concatenate([low, top], axis=axis)
    return lax.all_gather(value, "tensor", axis=axis, tiled=True)


def vec_mat(vec, mat):
    if vec.shape[0] == 1:
        return jnp.sum(vec[0][:, None] * mat, axis=0)[None]
    return jnp.einsum("bk,km->bm", vec, mat, precision=high)


def vec_mat_t(vec, mat):
    if vec.shape[0] == 1:
        return jnp.sum(vec[0][None, :] * mat, axis=1)[None]
    return jnp.einsum("bm,km->bk", vec, mat, precision=high)


def scattered_grad(left, right):
    tokens = left.shape[0] * left.shape[1]
    rows = left.shape[2]
    cols = right.shape[2]
    left_t = left.reshape(tokens, rows).T
    right = right.reshape(tokens, cols)
    count = lax.axis_size("dp")
    if count & count - 1 or count < 2:
        whole = jnp.dot(left_t, right, precision=high)
        return lax.psum_scatter(whole, "dp", scatter_dimension=0, tiled=True)
    block = rows // count
    index = lax.axis_index("dp")
    bit = index % 2
    blocks = left_t.reshape(count // 2, 2, block, tokens)

    def product(which):
        chosen = lax.dynamic_index_in_dim(blocks, which, 1, keepdims=False)
        return jnp.dot(chosen.reshape(rows // 2, tokens), right, precision=high)

    pairs = [(device, device ^ 1) for device in range(count)]
    arrived = lax.ppermute(product(1 - bit), "dp", pairs)
    total = product(bit) + arrived
    step = 2
    groups = count // 2
    while groups > 1:
        bit = index // step % 2
        parts = total.reshape(groups // 2, 2, block, cols)
        away = lax.dynamic_index_in_dim(parts, 1 - bit, 1, keepdims=False)
        kept = lax.dynamic_index_in_dim(parts, bit, 1, keepdims=False)
        pairs = [(device, device ^ step) for device in range(count)]
        total = kept + lax.ppermute(away, "dp", pairs)
        groups //= 2
        step *= 2
    return total.reshape(block, cols)


def on_device(
    inputs,
    condition,
    cotangent,
    w_qkv,
    b_qv,
    w_out,
    b_out,
    w_up,
    b_up,
    w_down,
    b_down,
    w_mod,
    b_mod,
):
    layers = w_qkv.shape[0]
    batch, seq_len, width = inputs.shape
    local_width = w_qkv.shape[3]
    heads_local = local_width // HEAD_DIM
    mod_cols = w_mod.shape[2]
    score_scale = HEAD_DIM ** (-0.5)
    activated = jax.nn.silu(condition)
    mod_local = (
        jnp.stack([vec_mat(activated, w_mod[index]) for index in range(layers)], axis=0)
        + b_mod[:, None, :]
    )
    mod_whole = pair_gather(mod_local, 2).reshape(layers, batch, 6, width)
    activated_all = lax.all_gather(activated, "dp", axis=0, tiled=True)
    kept = []
    hidden = inputs
    for layer_index in range(layers):
        modulation = mod_whole[layer_index]
        shift_a, scale_a, gate_a = (modulation[:, 0], modulation[:, 1], modulation[:, 2])
        shift_b, scale_b, gate_b = (modulation[:, 3], modulation[:, 4], modulation[:, 5])
        modul_a = layer_norm(hidden) * (1.0 + scale_a[:, None, :]) + shift_a[:, None, :]
        projected = jnp.einsum("bsd,dcm->bscm", modul_a, w_qkv[layer_index], precision=high)
        queries = (projected[:, :, 0] + b_qv[layer_index, 0]).reshape(
            batch, seq_len, heads_local, HEAD_DIM
        )
        keys = projected[:, :, 1].reshape(batch, seq_len, heads_local, HEAD_DIM)
        values = (projected[:, :, 2] + b_qv[layer_index, 1]).reshape(
            batch, seq_len, heads_local, HEAD_DIM
        )
        scores = jnp.einsum("bqhe,bkhe->bhqk", queries, keys, precision=high) * score_scale
        log_norm = jax.nn.logsumexp(scores, axis=-1, keepdims=True)
        probs = jnp.exp(scores - log_norm)
        attended = jnp.einsum("bhqk,bkhe->bqhe", probs, values, precision=high).reshape(
            batch, seq_len, local_width
        )
        partial_a = jnp.einsum("bsh,hd->bsd", attended, w_out[layer_index], precision=high)
        attn_branch = pair_sum(partial_a) + b_out[layer_index]
        middle = hidden + gate_a[:, None, :] * attn_branch
        modul_b = layer_norm(middle) * (1.0 + scale_b[:, None, :]) + shift_b[:, None, :]
        pre_act = (
            jnp.einsum("bsd,df->bsf", modul_b, w_up[layer_index], precision=high)
            + b_up[layer_index]
        )
        activ = gelu_tanh(pre_act)
        partial_b = jnp.einsum("bsf,fd->bsd", activ, w_down[layer_index], precision=high)
        mlp_branch = pair_sum(partial_b) + b_down[layer_index]
        result = middle + gate_b[:, None, :] * mlp_branch
        kept.append(
            (
                hidden,
                modul_a,
                queries,
                keys,
                values,
                probs,
                attended,
                attn_branch,
                middle,
                modul_b,
                pre_act,
                activ,
                mlp_branch,
            )
        )
        hidden = result
    grad_hidden = cotangent
    silu_grad_part = jnp.zeros((batch, width), jnp.float32)
    matrix_grads = [None] * layers
    pieces = [None] * layers
    for layer_index in reversed(range(layers)):
        (
            layer_in,
            modul_a,
            queries,
            keys,
            values,
            probs,
            attended,
            attn_branch,
            middle,
            modul_b,
            pre_act,
            activ,
            mlp_branch,
        ) = kept[layer_index]
        modulation = mod_whole[layer_index]
        scale_a, gate_a = (modulation[:, 1], modulation[:, 2])
        scale_b, gate_b = (modulation[:, 4], modulation[:, 5])
        d_branch_b = grad_hidden * gate_b[:, None, :]
        d_gate_b = jnp.sum(grad_hidden * mlp_branch, axis=1)
        g_b_down = jnp.sum(d_branch_b, axis=(0, 1))
        g_w_down = scattered_grad(d_branch_b, activ)
        d_activ = jnp.einsum("bsd,fd->bsf", d_branch_b, w_down[layer_index], precision=high)
        d_pre = jax.vjp(gelu_tanh, pre_act)[1](d_activ)[0]
        g_b_up = jnp.sum(d_pre, axis=(0, 1))
        g_w_up = scattered_grad(modul_b, d_pre)
        d_modul_b = pair_sum(jnp.einsum("bsf,df->bsd", d_pre, w_up[layer_index], precision=high))
        normed_b, norm_back_b = jax.vjp(layer_norm, middle)
        d_scale_b = jnp.sum(d_modul_b * normed_b, axis=1)
        d_shift_b = jnp.sum(d_modul_b, axis=1)
        d_middle = grad_hidden + norm_back_b(d_modul_b * (1.0 + scale_b[:, None, :]))[0]
        d_branch_a = d_middle * gate_a[:, None, :]
        d_gate_a = jnp.sum(d_middle * attn_branch, axis=1)
        g_b_out = jnp.sum(d_branch_a, axis=(0, 1))
        g_w_out = scattered_grad(d_branch_a, attended)
        d_attended = jnp.einsum(
            "bsd,hd->bsh", d_branch_a, w_out[layer_index], precision=high
        ).reshape(batch, seq_len, heads_local, HEAD_DIM)
        d_values = jnp.einsum("bhqk,bqhe->bkhe", probs, d_attended, precision=high)
        d_probs = jnp.einsum("bqhe,bkhe->bhqk", d_attended, values, precision=high)
        attended_heads = attended.reshape(batch, seq_len, heads_local, HEAD_DIM)
        row_dot = jnp.transpose(jnp.sum(d_attended * attended_heads, axis=-1), (0, 2, 1))[..., None]
        d_scores = probs * (d_probs - row_dot) * score_scale
        d_queries = jnp.einsum("bhqk,bkhe->bqhe", d_scores, keys, precision=high)
        d_keys = jnp.einsum("bhqk,bqhe->bkhe", d_scores, queries, precision=high)
        d_proj = jnp.stack([d_queries, d_keys, d_values], axis=2).reshape(
            batch, seq_len, 3, local_width
        )
        d_flat = d_proj.reshape(batch, seq_len, 3 * local_width)
        g_b_qv = jnp.sum(d_flat, axis=(0, 1))
        g_w_qkv = scattered_grad(modul_a, d_flat)
        d_modul_a = pair_sum(
            jnp.einsum("bscm,dcm->bsd", d_proj, w_qkv[layer_index], precision=high)
        )
        normed_a, norm_back_a = jax.vjp(layer_norm, layer_in)
        d_scale_a = jnp.sum(d_modul_a * normed_a, axis=1)
        d_shift_a = jnp.sum(d_modul_a, axis=1)
        grad_hidden = d_middle + norm_back_a(d_modul_a * (1.0 + scale_a[:, None, :]))[0]
        d_mod = jnp.stack(
            [d_shift_a, d_scale_a, d_gate_a, d_shift_b, d_scale_b, d_gate_b], axis=1
        ).reshape(batch, 6 * width)
        own_cols = lax.dynamic_slice_in_dim(d_mod, lax.axis_index("tensor") * mod_cols, mod_cols, 1)
        silu_grad_part = silu_grad_part + vec_mat_t(own_cols, w_mod[layer_index])
        matrix_grads[layer_index] = (g_w_qkv, g_w_out, g_w_up, g_w_down)
        pieces[layer_index] = (own_cols, (g_b_qv, g_b_out, g_b_up, g_b_down))
    block = width // lax.axis_size("dp")
    activated_rows = lax.dynamic_slice_in_dim(activated_all, lax.axis_index("dp") * block, block, 1)
    mod_grads = [None] * layers
    bias_grads = [None] * layers
    for layer_index in reversed(range(layers)):
        own_cols, biases = pieces[layer_index]
        line = jnp.concatenate(biases)[None]
        line = jnp.concatenate([line, jnp.zeros((batch - 1, line.shape[1]), line.dtype)], axis=0)
        gathered = lax.all_gather(
            jnp.concatenate([own_cols, line], axis=1), "dp", axis=0, tiled=True
        )
        mod_grads[layer_index] = jnp.einsum(
            "bd,bm->dm", activated_rows, gathered[:, :mod_cols], precision=high
        )
        sums = jnp.sum(gathered, axis=0)
        found = [sums[:mod_cols]]
        start = mod_cols
        for piece in biases:
            found.append(sums[start : start + piece.shape[0]])
            start += piece.shape[0]
        bias_grads[layer_index] = found
    order = range(layers)
    grad_w_qkv = jnp.stack([matrix_grads[index][0] for index in order], axis=0)
    grad_w_out = jnp.stack([matrix_grads[index][1].T for index in order], axis=0)
    grad_w_up = jnp.stack([matrix_grads[index][2] for index in order], axis=0)
    grad_w_down = jnp.stack([matrix_grads[index][3].T for index in order], axis=0)
    grad_b_mod, grad_b_qkv, grad_b_out, grad_b_up, grad_b_down = [
        jnp.stack([bias_grads[index][member] for index in order], axis=0) for member in range(5)
    ]
    grad_b_qv = grad_b_qkv.reshape(layers, 3, local_width)[:, ::2]
    grad_condition = pair_sum(silu_grad_part) * silu_slope(condition)
    return (
        hidden,
        grad_hidden,
        grad_condition,
        grad_w_qkv.reshape(layers, block, 3, local_width),
        grad_b_qv,
        grad_w_out,
        grad_b_out,
        grad_w_up,
        grad_b_up,
        grad_w_down,
        grad_b_down,
        jnp.stack(mod_grads, axis=0),
        grad_b_mod,
    )


def solution(mesh):
    in_specs = (
        P("dp", None, None),
        P("dp", None),
        P("dp", None, None),
        P(None, None, None, "tensor"),
        P(None, None, "tensor"),
        P(None, "tensor", None),
        P(),
        P(None, None, "tensor"),
        P(None, "tensor"),
        P(None, "tensor", None),
        P(),
        P(None, None, "tensor"),
        P(None, "tensor"),
    )
    out_specs = (
        P("dp", None, None),
        P("dp", None, None),
        P("dp", None),
        P(None, "dp", None, "tensor"),
        P(None, None, "tensor"),
        P(None, "tensor", "dp"),
        P(),
        P(None, "dp", "tensor"),
        P(None, "tensor"),
        P(None, "tensor", "dp"),
        P(),
        P(None, "dp", "tensor"),
        P(None, "tensor"),
    )
    return jax.shard_map(
        on_device, mesh=mesh, in_specs=in_specs, out_specs=out_specs, check_vma=False
    )
```

profile of v0, /device:TPU:0, one launch (start us, length us, event | category | flops | bytes accessed | tf_op | source)
XLA Modules:
  0.0 574.5 jit_solution(8802800314265596121)
XLA Ops:
  2.7 5.8 %fusion.2 = (f32[2304]{0:T(1024)S(1)}, f32[2304]{0:T(1024)S(1)}) fusion(f32[2,768,2304]{2,1,0:T(8,128)} %param.24, f32[768]{0:T(1024)S(1)} %multiply_reduce_fusion.20), kind=kLoop, calls=%fused_computation.6 | loop fusion | flops 7073280 | bytes 14177280 | tf_op jit(solution)/shard_map/reduce_sum | solution.py:45
  14.8 4.0 fusion.62
  26.7 15.8 %collective-permute-done.1 = f32[1,256,768]{2,1,0:T(8,128)S(1)} collective-permute-done((f32[1,256,768]{2,1,0:T(8,128)S(1)}, f32[1,256,768]{2,1,0:T(8,128)S(1)}, u32[]{:S(2)}, u32[]{:S(2)}) %collective-permute-start.1) | collective-permute-done | bytes 786464 | tf_op jit(solution)/shard_map/ppermute | solution.py:29
  44.2 4.7 fusion.40
  48.9 5.5 fusion.77
  59.7 13.0 %collective-permute-done.2 = f32[1,256,768]{2,1,0:T(8,128)} collective-permute-done((f32[1,256,768]{2,1,0:T(8,128)S(1)}, f32[1,256,768]{2,1,0:T(8,128)}, u32[]{:S(2)}, u32[]{:S(2)}) %collective-permute-start.2) | collective-permute-done | bytes 786464 | tf_op jit(solution)/shard_map/ppermute | solution.py:29
  74.9 15.7 %fusion.65 = f32[1,256,3,384]{3,1,2,0:T(8,128)S(1)} fusion(f32[2,768,3,384]{3,1,2,0:T(8,128)} %param.16, f32[1,256,768]{2,1,0:T(8,128)S(1)} %get-tuple-element.127, f32[768]{0:T(1024)S(1)} %copy-done.114, f32[768]{0:T(1024)S(1)} %copy-done.96, f32[256]{0:T(256)S(1)} %fusion.180, f32[256]{0:T(256)S(1)} %broadcast_multiply_fusion.1), kind=kOutput, calls=%fused_computation.81 | convolution fusion | flops 1359740928 | bytes 5513216 | tf_op jit(solution)/shard_map/bsd,dcm->bscm/dot_general | solution.py:126
  102.2 21.9 %all-gather.2 = f32[16,1,768]{2,1,0:T(1,128)S(1)} all-gather(f32[1,1,768]{2,1,0:T(1,128)} %get-tuple-element.100), channel_id=1, replica_groups=mesh['dp'=16,'tensor'=2] {'dp'}, dimensions={0}, use_global_device_ids=true | all-gather | bytes 52224 | tf_op jit(solution)/shard_map/all_gather | solution.py:118
  126.3 4.9 fusion.43
  131.3 6.3 %fusion.206 = (f32[1536]{0:T(1024)}, f32[256,1536]{1,0:T(8,128)S(1)}) fusion(f32[256,1536]{1,0:T(8,128)S(1)} %fusion.43, f32[2,1536,768]{2,1,0:T(8,128)} %param.22, f32[1,256,768]{2,1,0:T(8,128)S(1)} %copy-done.64, f32[768]{0:T(1024)S(1)} %copy-done.154), kind=kOutput, calls=%fused_computation.396 | convolution fusion | flops 1819998720 | bytes 8659968 | tf_op jit(solution)/shard_map/bsd,fd->bsf/dot_general | solution.py:197
  142.9 5.6 fusion.83
  150.5 11.1 %collective-permute-done.5 = f32[1,256,768]{2,1,0:T(8,128)} collective-permute-done((f32[1,256,768]{2,1,0:T(8,128)}, f32[1,256,768]{2,1,0:T(8,128)}, u32[]{:S(2)}, u32[]{:S(2)}) %collective-permute-start.5) | collective-permute-done | bytes 786464 | tf_op jit(solution)/shard_map/ppermute | solution.py:29
  163.9 13.8 %collective-permute-done.4 = f32[1,256,768]{2,1,0:T(8,128)S(1)} collective-permute-done((f32[1,256,768]{2,1,0:T(8,128)S(1)}, f32[1,256,768]{2,1,0:T(8,128)S(1)}, u32[]{:S(2)}, u32[]{:S(2)}) %collective-permute-start.4) | collective-permute-done | bytes 786464 | tf_op jit(solution)/shard_map/ppermute | solution.py:29
  191.5 4.7 fusion.71
  230.6 6.0 %fusion.207 = (f32[1536]{0:T(1024)}, f32[256,1536]{1,0:T(8,128)S(1)}) fusion(f32[256,1536]{1,0:T(8,128)S(1)} %copy-done.7, f32[2,1536,768]{2,1,0:T(8,128)} %param.22, f32[1,256,768]{2,1,0:T(8,128)S(1)} %get-tuple-element.168, f32[768]{0:T(1024)S(1)} %copy-done.92), kind=kOutput, calls=%fused_computation.397 | convolution fusion | flops 1819998720 | bytes 8659968 | tf_op jit(solution)/shard_map/bsd,fd->bsf/dot_general | solution.py:197
  246.0 21.6 %all-gather.1 = f32[16,1,6528]{2,1,0:T(1,128)} all-gather(f32[1,1,6528]{2,1,0:T(1,128)S(1)} %maximum_bitcast_fusion.1), channel_id=1, replica_groups=mesh['dp'=16,'tensor'=2] {'dp'}, dimensions={0}, use_global_device_ids=true | all-gather | bytes 443904 | tf_op jit(solution)/shard_map/all_gather | solution.py:248
  293.6 5.0 collective-permute-done.25
  312.0 4.8 fusion.68
  330.7 5.6 collective-permute-done.8
  341.4 18.7 %all-gather = f32[16,1,6528]{2,1,0:T(1,128)S(1)} all-gather(f32[1,1,6528]{2,1,0:T(1,128)S(1)} %maximum_bitcast_fusion), channel_id=1, replica_groups=mesh['dp'=16,'tensor'=2] {'dp'}, dimensions={0}, use_global_device_ids=true | all-gather | bytes 443904 | tf_op jit(solution)/shard_map/all_gather | solution.py:248
  361.2 5.9 %fusion.3 = (f32[768]{0:T(1024)S(1)}, f32[768]{0:T(1024)S(1)}) fusion(f32[2,768,2304]{2,1,0:T(8,128)} %param.24, f32[2304]{0:T(1024)S(1)} %get-tuple-element.110, f32[2304]{0:T(1024)S(1)} %copy-done.100), kind=kLoop, calls=%fused_computation.7 | loop fusion | flops 7076352 | bytes 14180352 | tf_op jit(solution)/shard_map/reduce_sum | solution.py:51
  394.1 5.7 collective-permute-done.21
  405.8 29.7 %collective-permute-done.15 = f32[4,48,1152]{2,1,0:T(8,128)S(1)} collective-permute-done((f32[4,48,1152]{2,1,0:T(8,128)S(1)}, f32[4,48,1152]{2,1,0:T(8,128)S(1)}, u32[]{:S(2)}, u32[]{:S(2)}) %collective-permute-start.15) | collective-permute-done | bytes 884768 | tf_op jit(solution)/shard_map/ppermute | solution.py:85
  436.5 24.4 %collective-permute-done.31 = f32[4,48,1536]{2,1,0:T(8,128)S(1)} collective-permute-done((f32[4,48,1536]{2,1,0:T(8,128)S(1)}, f32[4,48,1536]{2,1,0:T(8,128)S(1)}, u32[]{:S(2)}, u32[]{:S(2)}) %collective-permute-start.31) | collective-permute-done | bytes 1179680 | tf_op jit(solution)/shard_map/ppermute | solution.py:85
  466.3 23.2 %collective-permute-done.17 = f32[1,48,1152]{2,1,0:T(8,128)S(1)} collective-permute-done((f32[1,48,1152]{2,1,0:T(8,128)S(1)}, f32[1,48,1152]{2,1,0:T(8,128)S(1)}, u32[]{:S(2)}, u32[]{:S(2)}) %collective-permute-start.17) | collective-permute-done | bytes 221216 | tf_op jit(solution)/shard_map/ppermute | solution.py:85
  497.9 13.5 %collective-permute-done.41 = f32[1,48,1536]{2,1,0:T(8,128)S(1)} collective-permute-done((f32[1,48,1536]{2,1,0:T(8,128)S(1)}, f32[1,48,1536]{2,1,0:T(8,128)S(1)}, u32[]{:S(2)}, u32[]{:S(2)}) %collective-permute-start.41) | collective-permute-done | bytes 294944 | tf_op jit(solution)/shard_map/ppermute | solution.py:85
  511.4 5.5 collective-permute-done.33
  517.0 3.6 collective-permute-done.36
  520.7 13.3 %collective-permute-done.11 = f32[4,48,1152]{2,1,0:T(8,128)S(1)} collective-permute-done((f32[4,48,1152]{2,1,0:T(8,128)S(1)}, f32[4,48,1152]{2,1,0:T(8,128)S(1)}, u32[]{:S(2)}, u32[]{:S(2)}) %collective-permute-start.11) | collective-permute-done | bytes 884768 | tf_op jit(solution)/shard_map/ppermute | solution.py:85
  537.4 12.3 %collective-permute-done.12 = f32[2,48,1152]{2,1,0:T(8,128)S(1)} collective-permute-done((f32[2,48,1152]{2,1,0:T(8,128)S(1)}, f32[2,48,1152]{2,1,0:T(8,128)S(1)}, u32[]{:S(2)}, u32[]{:S(2)}) %collective-permute-start.12) | collective-permute-done | bytes 442400 | tf_op jit(solution)/shard_map/ppermute | solution.py:85
  550.6 11.2 %collective-permute-done.28 = f32[2,48,1536]{2,1,0:T(8,128)S(1)} collective-permute-done((f32[2,48,1536]{2,1,0:T(8,128)S(1)}, f32[2,48,1536]{2,1,0:T(8,128)S(1)}, u32[]{:S(2)}, u32[]{:S(2)}) %collective-permute-start.28) | collective-permute-done | bytes 589856 | tf_op jit(solution)/shard_map/ppermute | solution.py:85
  564.1 9.4 %collective-permute-done.29 = f32[1,48,1536]{2,1,0:T(8,128)S(1)} collective-permute-done((f32[1,48,1536]{2,1,0:T(8,128)S(1)}, f32[1,48,1536]{2,1,0:T(8,128)S(1)}, u32[]{:S(2)}, u32[]{:S(2)}) %collective-permute-start.29) | collective-permute-done | bytes 294944 | tf_op jit(solution)/shard_map/ppermute | solution.py:85
  (673 shorter events, 219.0 us)
Async XLA Ops:
  23.4 19.1 %collective-permute-start.1 = (f32[1,256,768]{2,1,0:T(8,128)S(1)}, f32[1,256,768]{2,1,0:T(8,128)S(1)}, u32[]{:S(2)}, u32[]{:S(2)}) collective-permute-start(f32[1,256,768]{2,1,0:T(8,128)S(1)} %convolution_bitcast_fusion.3), channel_id=1, source_target_pairs={{0,1},{1,0},{2,3},{3,2},{4,5},{5,4},{6,7},{7,6},{8,9},{9,8},{10,11... | collective-permute-start | bytes 2359304 | tf_op jit(solution)/shard_map/ppermute | solution.py:29
  54.4 18.3 %collective-permute-start.2 = (f32[1,256,768]{2,1,0:T(8,128)S(1)}, f32[1,256,768]{2,1,0:T(8,128)}, u32[]{:S(2)}, u32[]{:S(2)}) collective-permute-start(f32[1,256,768]{2,1,0:T(8,128)S(1)} %fusion.77), channel_id=1, source_target_pairs={{0,1},{1,0},{2,3},{3,2},{4,5},{5,4},{6,7},{7,6},{8,9},{9,8},{10,11... | collective-permute-start | bytes 2359304 | tf_op jit(solution)/shard_map/ppermute | solution.py:29
  101.9 22.2 %collective-permute-start.3 = (f32[1,256,768]{2,1,0:T(8,128)}, f32[1,256,768]{2,1,0:T(8,128)}, u32[]{:S(2)}, u32[]{:S(2)}) collective-permute-start(f32[1,256,768]{2,1,0:T(8,128)} %convolution_bitcast_fusion.2), channel_id=1, source_target_pairs={{0,1},{1,0},{2,3},{3,2},{4,5},{5,4},{6,7},{7,6},{8,9},{9,8},{10,11... | collective-permute-start | bytes 2359304 | tf_op jit(solution)/shard_map/ppermute | solution.py:29
  140.9 20.7 %collective-permute-start.5 = (f32[1,256,768]{2,1,0:T(8,128)}, f32[1,256,768]{2,1,0:T(8,128)}, u32[]{:S(2)}, u32[]{:S(2)}) collective-permute-start(f32[1,256,768]{2,1,0:T(8,128)} %fusion.80), channel_id=1, source_target_pairs={{0,1},{1,0},{2,3},{3,2},{4,5},{5,4},{6,7},{7,6},{8,9},{9,8},{10,11... | collective-permute-start | bytes 2359304 | tf_op jit(solution)/shard_map/ppermute | solution.py:29
  148.5 29.3 %collective-permute-start.4 = (f32[1,256,768]{2,1,0:T(8,128)S(1)}, f32[1,256,768]{2,1,0:T(8,128)S(1)}, u32[]{:S(2)}, u32[]{:S(2)}) collective-permute-start(f32[1,256,768]{2,1,0:T(8,128)S(1)} %fusion.83), channel_id=1, source_target_pairs={{0,1},{1,0},{2,3},{3,2},{4,5},{5,4},{6,7},{7,6},{8,9},{9,8},{10,11... | collective-permute-start | bytes 2359304 | tf_op jit(solution)/shard_map/ppermute | solution.py:29
  196.2 27.9 %collective-permute-start.6 = (f32[1,256,768]{2,1,0:T(8,128)}, f32[1,256,768]{2,1,0:T(8,128)}, u32[]{:S(2)}, u32[]{:S(2)}) collective-permute-start(f32[1,256,768]{2,1,0:T(8,128)} %fusion.71), channel_id=1, source_target_pairs={{0,1},{1,0},{2,3},{3,2},{4,5},{5,4},{6,7},{7,6},{8,9},{9,8},{10,11... | collective-permute-start | bytes 2359304 | tf_op jit(solution)/shard_map/ppermute | solution.py:29
  214.0 163.1 %collective-permute-start.38 = (f32[384,1536]{1,0:T(8,128)}, f32[384,1536]{1,0:T(8,128)}, u32[]{:S(2)}, u32[]{:S(2)}) collective-permute-start(f32[384,1536]{1,0:T(8,128)} %fusion.187), channel_id=1, source_target_pairs={{0,2},{2,0},{4,6},{6,4},{8,10},{10,8},{12,14},{14,12},{16,18},{18,... | collective-permute-start | bytes 7077896 | tf_op jit(solution)/shard_map/ppermute | solution.py:75
  221.5 160.6 %collective-permute-start.30 = (f32[384,1536]{1,0:T(8,128)}, f32[384,1536]{1,0:T(8,128)}, u32[]{:S(2)}, u32[]{:S(2)}) collective-permute-start(f32[384,1536]{1,0:T(8,128)} %fusion.215), channel_id=1, source_target_pairs={{0,2},{2,0},{4,6},{6,4},{8,10},{10,8},{12,14},{14,12},{16,18},{18,... | collective-permute-start | bytes 7077896 | tf_op jit(solution)/shard_map/ppermute | solution.py:75
  224.1 59.1 %collective-permute-start.23 = (f32[4,48,384]{2,1,0:T(8,128)}, f32[4,48,384]{2,1,0:T(8,128)}, u32[]{:S(2)}, u32[]{:S(2)}) collective-permute-start(f32[4,48,384]{2,1,0:T(8,128)} %dynamic-slice_bitcast_fusion.12), channel_id=1, source_target_pairs={{0,4},{2,6},{4,0},{6,2},{8,12},{10,14},{12,8},{14,10},{16,20},{18,... | collective-permute-start | bytes 884744 | tf_op jit(solution)/shard_map/ppermute | solution.py:85
  240.0 59.3 %collective-permute-start.7 = (f32[1,256,768]{2,1,0:T(8,128)}, f32[1,256,768]{2,1,0:T(8,128)}, u32[]{:S(2)}, u32[]{:S(2)}) collective-permute-start(f32[1,256,768]{2,1,0:T(8,128)} %fusion.74), channel_id=1, source_target_pairs={{0,1},{1,0},{2,3},{3,2},{4,5},{5,4},{6,7},{7,6},{8,9},{9,8},{10,11... | collective-permute-start | bytes 2359304 | tf_op jit(solution)/shard_map/ppermute | solution.py:29
  286.3 115.7 %collective-permute-start.34 = (f32[384,1536]{1,0:T(8,128)}, f32[384,1536]{1,0:T(8,128)}, u32[]{:S(2)}, u32[]{:S(2)}) collective-permute-start(f32[384,1536]{1,0:T(8,128)} %fusion.186), channel_id=1, source_target_pairs={{0,2},{2,0},{4,6},{6,4},{8,10},{10,8},{12,14},{14,12},{16,18},{18,... | collective-permute-start | bytes 7077896 | tf_op jit(solution)/shard_map/ppermute | solution.py:75
  316.8 19.5 %collective-permute-start.8 = (f32[1,256,768]{2,1,0:T(8,128)}, f32[1,256,768]{2,1,0:T(8,128)}, u32[]{:S(2)}, u32[]{:S(2)}) collective-permute-start(f32[1,256,768]{2,1,0:T(8,128)} %fusion.68), channel_id=1, source_target_pairs={{0,1},{1,0},{2,3},{3,2},{4,5},{5,4},{6,7},{7,6},{8,9},{9,8},{10,11... | collective-permute-start | bytes 2359304 | tf_op jit(solution)/shard_map/ppermute | solution.py:29
  328.5 59.8 %collective-permute-start.14 = (f32[384,1152]{1,0:T(8,128)}, f32[384,1152]{1,0:T(8,128)}, u32[]{:S(2)}, u32[]{:S(2)}) collective-permute-start(f32[384,1152]{1,0:T(8,128)} %fusion.211), channel_id=1, source_target_pairs={{0,2},{2,0},{4,6},{6,4},{8,10},{10,8},{12,14},{14,12},{16,18},{18,... | collective-permute-start | bytes 5308424 | tf_op jit(solution)/shard_map/ppermute | solution.py:75
  336.2 127.0 %collective-permute-start.26 = (f32[384,1536]{1,0:T(8,128)}, f32[384,1536]{1,0:T(8,128)}, u32[]{:S(2)}, u32[]{:S(2)}) collective-permute-start(f32[384,1536]{1,0:T(8,128)} %fusion.214), channel_id=1, source_target_pairs={{0,2},{2,0},{4,6},{6,4},{8,10},{10,8},{12,14},{14,12},{16,18},{18,... | collective-permute-start | bytes 7077896 | tf_op jit(solution)/shard_map/ppermute | solution.py:75
  386.6 107.3 %collective-permute-start.10 = (f32[384,1152]{1,0:T(8,128)S(1)}, f32[384,1152]{1,0:T(8,128)S(1)}, u32[]{:S(2)}, u32[]{:S(2)}) collective-permute-start(f32[384,1152]{1,0:T(8,128)S(1)} %fusion.210), channel_id=1, source_target_pairs={{0,2},{2,0},{4,6},{6,4},{8,10},{10,8},{12,14},{14,12},{16,18},{18,... | collective-permute-start | bytes 5308424 | tf_op jit(solution)/shard_map/ppermute | solution.py:75
  387.7 48.4 %collective-permute-start.39 = (f32[4,48,1536]{2,1,0:T(8,128)S(1)}, f32[4,48,1536]{2,1,0:T(8,128)S(1)}, u32[]{:S(2)}, u32[]{:S(2)}) collective-permute-start(f32[4,48,1536]{2,1,0:T(8,128)S(1)} %dynamic-slice_bitcast_fusion), channel_id=1, source_target_pairs={{0,4},{2,6},{4,0},{6,2},{8,12},{10,14},{12,8},{14,10},{16,20},{18,... | collective-permute-start | bytes 3538952 | tf_op jit(solution)/shard_map/ppermute | solution.py:85
  399.8 35.8 %collective-permute-start.15 = (f32[4,48,1152]{2,1,0:T(8,128)S(1)}, f32[4,48,1152]{2,1,0:T(8,128)S(1)}, u32[]{:S(2)}, u32[]{:S(2)}) collective-permute-start(f32[4,48,1152]{2,1,0:T(8,128)S(1)} %dynamic-slice_bitcast_fusion.4), channel_id=1, source_target_pairs={{0,4},{2,6},{4,0},{6,2},{8,12},{10,14},{12,8},{14,10},{16,20},{18,... | collective-permute-start | bytes 2654216 | tf_op jit(solution)/shard_map/ppermute | solution.py:85
  402.0 58.8 %collective-permute-start.31 = (f32[4,48,1536]{2,1,0:T(8,128)S(1)}, f32[4,48,1536]{2,1,0:T(8,128)S(1)}, u32[]{:S(2)}, u32[]{:S(2)}) collective-permute-start(f32[4,48,1536]{2,1,0:T(8,128)S(1)} %dynamic-slice_bitcast_fusion.2), channel_id=1, source_target_pairs={{0,4},{2,6},{4,0},{6,2},{8,12},{10,14},{12,8},{14,10},{16,20},{18,... | collective-permute-start | bytes 3538952 | tf_op jit(solution)/shard_map/ppermute | solution.py:85
  435.5 61.1 %collective-permute-start.35 = (f32[4,48,1536]{2,1,0:T(8,128)S(1)}, f32[4,48,1536]{2,1,0:T(8,128)S(1)}, u32[]{:S(2)}, u32[]{:S(2)}) collective-permute-start(f32[4,48,1536]{2,1,0:T(8,128)S(1)} %dynamic-slice_bitcast_fusion.1), channel_id=1, source_target_pairs={{0,4},{2,6},{4,0},{6,2},{8,12},{10,14},{12,8},{14,10},{16,20},{18,... | collective-permute-start | bytes 3538952 | tf_op jit(solution)/shard_map/ppermute | solution.py:85
  436.2 24.9 %collective-permute-start.16 = (f32[2,48,1152]{2,1,0:T(8,128)S(1)}, f32[2,48,1152]{2,1,0:T(8,128)S(1)}, u32[]{:S(2)}, u32[]{:S(2)}) collective-permute-start(f32[2,48,1152]{2,1,0:T(8,128)S(1)} %dynamic-slice_bitcast_fusion.10), channel_id=1, source_target_pairs={{0,8},{2,10},{4,12},{6,14},{8,0},{10,2},{12,4},{14,6},{16,24},{18,... | collective-permute-start | bytes 1327112 | tf_op jit(solution)/shard_map/ppermute | solution.py:85
  460.8 29.2 %collective-permute-start.40 = (f32[2,48,1536]{2,1,0:T(8,128)S(1)}, f32[2,48,1536]{2,1,0:T(8,128)S(1)}, u32[]{:S(2)}, u32[]{:S(2)}) collective-permute-start(f32[2,48,1536]{2,1,0:T(8,128)S(1)} %dynamic-slice_bitcast_fusion.6), channel_id=1, source_target_pairs={{0,8},{2,10},{4,12},{6,14},{8,0},{10,2},{12,4},{14,6},{16,24},{18,... | collective-permute-start | bytes 1769480 | tf_op jit(solution)/shard_map/ppermute | solution.py:85
  461.0 32.7 %collective-permute-start.32 = (f32[2,48,1536]{2,1,0:T(8,128)S(1)}, f32[2,48,1536]{2,1,0:T(8,128)S(1)}, u32[]{:S(2)}, u32[]{:S(2)}) collective-permute-start(f32[2,48,1536]{2,1,0:T(8,128)S(1)} %dynamic-slice_bitcast_fusion.8), channel_id=1, source_target_pairs={{0,8},{2,10},{4,12},{6,14},{8,0},{10,2},{12,4},{14,6},{16,24},{18,... | collective-permute-start | bytes 1769480 | tf_op jit(solution)/shard_map/ppermute | solution.py:85
  463.2 26.3 %collective-permute-start.17 = (f32[1,48,1152]{2,1,0:T(8,128)S(1)}, f32[1,48,1152]{2,1,0:T(8,128)S(1)}, u32[]{:S(2)}, u32[]{:S(2)}) collective-permute-start(f32[1,48,1152]{2,1,0:T(8,128)S(1)} %constant_dynamic-slice_fusion.19), channel_id=1, source_target_pairs={{0,16},{2,18},{4,20},{6,22},{8,24},{10,26},{12,28},{14,30},{16,0},... | collective-permute-start | bytes 663560 | tf_op jit(solution)/shard_map/ppermute | solution.py:85
  489.5 46.0 %collective-permute-start.27 = (f32[4,48,1536]{2,1,0:T(8,128)S(1)}, f32[4,48,1536]{2,1,0:T(8,128)S(1)}, u32[]{:S(2)}, u32[]{:S(2)}) collective-permute-start(f32[4,48,1536]{2,1,0:T(8,128)S(1)} %dynamic-slice_bitcast_fusion.3), channel_id=1, source_target_pairs={{0,4},{2,6},{4,0},{6,2},{8,12},{10,14},{12,8},{14,10},{16,20},{18,... | collective-permute-start | bytes 3538952 | tf_op jit(solution)/shard_map/ppermute | solution.py:85
  490.2 21.2 %collective-permute-start.41 = (f32[1,48,1536]{2,1,0:T(8,128)S(1)}, f32[1,48,1536]{2,1,0:T(8,128)S(1)}, u32[]{:S(2)}, u32[]{:S(2)}) collective-permute-start(f32[1,48,1536]{2,1,0:T(8,128)S(1)} %constant_dynamic-slice_fusion.1), channel_id=1, source_target_pairs={{0,16},{2,18},{4,20},{6,22},{8,24},{10,26},{12,28},{14,30},{16,0},... | collective-permute-start | bytes 884744 | tf_op jit(solution)/shard_map/ppermute | solution.py:85
  493.8 23.1 %collective-permute-start.33 = (f32[1,48,1536]{2,1,0:T(8,128)S(1)}, f32[1,48,1536]{2,1,0:T(8,128)S(1)}, u32[]{:S(2)}, u32[]{:S(2)}) collective-permute-start(f32[1,48,1536]{2,1,0:T(8,128)S(1)} %constant_dynamic-slice_fusion.7), channel_id=1, source_target_pairs={{0,16},{2,18},{4,20},{6,22},{8,24},{10,26},{12,28},{14,30},{16,0},... | collective-permute-start | bytes 884744 | tf_op jit(solution)/shard_map/ppermute | solution.py:85
  495.0 39.0 %collective-permute-start.11 = (f32[4,48,1152]{2,1,0:T(8,128)S(1)}, f32[4,48,1152]{2,1,0:T(8,128)S(1)}, u32[]{:S(2)}, u32[]{:S(2)}) collective-permute-start(f32[4,48,1152]{2,1,0:T(8,128)S(1)} %dynamic-slice_bitcast_fusion.5), channel_id=1, source_target_pairs={{0,4},{2,6},{4,0},{6,2},{8,12},{10,14},{12,8},{14,10},{16,20},{18,... | collective-permute-start | bytes 2654216 | tf_op jit(solution)/shard_map/ppermute | solution.py:85
  496.8 23.7 %collective-permute-start.36 = (f32[2,48,1536]{2,1,0:T(8,128)S(1)}, f32[2,48,1536]{2,1,0:T(8,128)S(1)}, u32[]{:S(2)}, u32[]{:S(2)}) collective-permute-start(f32[2,48,1536]{2,1,0:T(8,128)S(1)} %dynamic-slice_bitcast_fusion.7), channel_id=1, source_target_pairs={{0,8},{2,10},{4,12},{6,14},{8,0},{10,2},{12,4},{14,6},{16,24},{18,... | collective-permute-start | bytes 1769480 | tf_op jit(solution)/shard_map/ppermute | solution.py:85
  520.7 15.8 %collective-permute-start.37 = (f32[1,48,1536]{2,1,0:T(8,128)S(1)}, f32[1,48,1536]{2,1,0:T(8,128)S(1)}, u32[]{:S(2)}, u32[]{:S(2)}) collective-permute-start(f32[1,48,1536]{2,1,0:T(8,128)S(1)} %constant_dynamic-slice_fusion.4), channel_id=1, source_target_pairs={{0,16},{2,18},{4,20},{6,22},{8,24},{10,26},{12,28},{14,30},{16,0},... | collective-permute-start | bytes 884744 | tf_op jit(solution)/shard_map/ppermute | solution.py:85
  534.1 15.5 %collective-permute-start.12 = (f32[2,48,1152]{2,1,0:T(8,128)S(1)}, f32[2,48,1152]{2,1,0:T(8,128)S(1)}, u32[]{:S(2)}, u32[]{:S(2)}) collective-permute-start(f32[2,48,1152]{2,1,0:T(8,128)S(1)} %dynamic-slice_bitcast_fusion.11), channel_id=1, source_target_pairs={{0,8},{2,10},{4,12},{6,14},{8,0},{10,2},{12,4},{14,6},{16,24},{18,... | collective-permute-start | bytes 1327112 | tf_op jit(solution)/shard_map/ppermute | solution.py:85
  535.7 26.0 %collective-permute-start.28 = (f32[2,48,1536]{2,1,0:T(8,128)S(1)}, f32[2,48,1536]{2,1,0:T(8,128)S(1)}, u32[]{:S(2)}, u32[]{:S(2)}) collective-permute-start(f32[2,48,1536]{2,1,0:T(8,128)S(1)} %dynamic-slice_bitcast_fusion.9), channel_id=1, source_target_pairs={{0,8},{2,10},{4,12},{6,14},{8,0},{10,2},{12,4},{14,6},{16,24},{18,... | collective-permute-start | bytes 1769480 | tf_op jit(solution)/shard_map/ppermute | solution.py:85
  549.8 13.4 %collective-permute-start.13 = (f32[1,48,1152]{2,1,0:T(8,128)S(1)}, f32[1,48,1152]{2,1,0:T(8,128)S(1)}, u32[]{:S(2)}, u32[]{:S(2)}) collective-permute-start(f32[1,48,1152]{2,1,0:T(8,128)S(1)} %constant_dynamic-slice_fusion.22), channel_id=1, source_target_pairs={{0,16},{2,18},{4,20},{6,22},{8,24},{10,26},{12,28},{14,30},{16,0},... | collective-permute-start | bytes 663560 | tf_op jit(solution)/shard_map/ppermute | solution.py:85
  (192 other events, 1133.6 us)
where the time goes:
time: 585 us; the launch traced here: 575 us
  waiting for transfers between devices  222 us (38%)
  matrix products  126 us (22%)
  local copies, waits for them, and re-layouts  68.9 us (12%)
  blocking collectives  62.3 us (11%)
  other arithmetic  58.5 us (10%)
  starting transfers between devices  33 us (6%)
    ppermute x24, waiting for transfers between devices, scattered_grad(): total = kept + lax.ppermute(away, 'dp', pairs)  163 us
    ppermute x9, waiting for transfers between devices, pair_sum(): return value + lax.ppermute(value, 'tensor', [(0, 1), (1, 0)])  59.2 us
    all_gather x2, blocking collectives, on_device(): lax.all_gather(jnp.concatenate([own_cols, line], axis=1), 'dp', axis=0, t...  40.3 us
    dot_general x16, matrix products, product(): return jnp.dot(chosen.reshape(rows // 2, tokens), right, precision=high)  35.7 us
    all_gather x1, blocking collectives, on_device(): activated_all = lax.all_gather(activated, 'dp', axis=0, tiled=True)  21.9 us
    dot_general x2, matrix products, on_device(): jnp.einsum('bsd,dcm->bscm', modul_a, w_qkv[layer_index], precision=high)  19.6 us
    ppermute x24, starting transfers between devices, scattered_grad(): total = kept + lax.ppermute(away, 'dp', pairs)  18.2 us
    transpose x8, local copies, waits for them, and re-layouts, scattered_grad(): left_t = left.reshape(tokens, rows).T  15.7 us
  transfers between devices with their start and end apart: 42, of which 19 were waited for; matrix products, arithmetic and copies ran while one was open for 27% of the time, Pallas kernels for 0%

commit v1 on v0

--- a/solution.py
+++ b/solution.py
@@ -2,10 +2,31 @@
 import jax.numpy as jnp
 from jax import lax
 from jax.sharding import PartitionSpec as P
+from jax.lax import axis_index, ppermute, psum
 
 HEAD_DIM = 64
 high = lax.Precision.HIGH
 eps_norm = 1e-06
+
+
+def find_chunk(z, across):
+    kept_arr = psum(1, axis_name=across)
+    tmp, aux, spare = (kept_arr, axis_index(across), z.shape[0])
+    step_out, e_next = (z, 1)
+    while e_next < tmp:
+        step_out = jnp.concatenate(
+            [
+                step_out,
+                ppermute(
+                    step_out,
+                    axis_name=across,
+                    perm=tuple(((idx, (idx - e_next) % tmp) for idx in range(tmp))),
+                ),
+            ],
+            0,
+        )
+        e_next = 2 * e_next
+    return jnp.roll(step_out, aux * spare, 0)
 
 
 def layer_norm(values):
@@ -245,9 +266,7 @@
         own_cols, biases = pieces[layer_index]
         line = jnp.concatenate(biases)[None]
         line = jnp.concatenate([line, jnp.zeros((batch - 1, line.shape[1]), line.dtype)], axis=0)
-        gathered = lax.all_gather(
-            jnp.concatenate([own_cols, line], axis=1), "dp", axis=0, tiled=True
-        )
+        gathered = find_chunk(jnp.concatenate([own_cols, line], axis=1), "dp")
         mod_grads[layer_index] = jnp.einsum(
             "bd,bm->dm", activated_rows, gathered[:, :mod_cols], precision=high
         )

time: 585 us -> 640 us (1.094)
  waiting for transfers between devices: 222 us -> 321 us
  blocking collectives: 62.3 us -> 20.7 us
  matrix products: 126 us -> 115 us
  starting transfers between devices: 33 us -> 43.8 us
    ppermute x24, waiting for transfers between devices: 163 us -> 223 us  [scattered_grad(): total = kept + lax.ppermute(away, 'dp', pairs)]
    all_gather x2 -> x0, blocking collectives: 40.3 us -> none  [on_device(): lax.all_gather(jnp.concatenate([own_cols, line], axis=1), 'dp', axis=0, t...]
    ppermute x0 -> x8, waiting for transfers between devices: none -> 22.7 us  [find_chunk(): ppermute(step_out, axis_name=across, perm=tuple(((idx, (idx - e_next) % t...]
    ppermute x9, waiting for transfers between devices: 59.2 us -> 75.1 us  [pair_sum(): return value + lax.ppermute(value, 'tensor', [(0, 1), (1, 0)])]
    dot_general x2, matrix products: 19.6 us -> 8.16 us  [on_device(): jnp.einsum('bsd,dcm->bscm', modul_a, w_qkv[layer_index], precision=high)]
    ppermute x0 -> x8, starting transfers between devices: none -> 9.27 us  [find_chunk(): ppermute(step_out, axis_name=across, perm=tuple(((idx, (idx - e_next) % t...]
    dynamic_slice x8 -> x4, local copies, waits for them, and re-layouts: 13 us -> 6.01 us  [product(): chosen = lax.dynamic_index_in_dim(blocks, which, 1, keepdims=False)]
  transfers between devices with their start and end apart: 42 -> 50, of which waited for: 19 -> 31; matrix products, arithmetic and copies ran while one was open for 27% -> 23% of each run, Pallas kernels for 0% -> 0%
where the time goes in v1:
time: 640 us; the launch traced here: 629 us
  waiting for transfers between devices  321 us (50%)
  matrix products  115 us (18%)
  local copies, waits for them, and re-layouts  67.4 us (11%)
  other arithmetic  57.5 us (9%)
  starting transfers between devices  43.8 us (7%)
  blocking collectives  20.7 us (3%)
    ppermute x24, waiting for transfers between devices, scattered_grad(): total = kept + lax.ppermute(away, 'dp', pairs)  223 us
    ppermute x9, waiting for transfers between devices, pair_sum(): return value + lax.ppermute(value, 'tensor', [(0, 1), (1, 0)])  75.1 us
    dot_general x16, matrix products, product(): return jnp.dot(chosen.reshape(rows // 2, tokens), right, precision=high)  33.3 us
    ppermute x8, waiting for transfers between devices, find_chunk(): ppermute(step_out, axis_name=across, perm=tuple(((idx, (idx - e_next) % t...  22.7 us
    ppermute x24, starting transfers between devices, scattered_grad(): total = kept + lax.ppermute(away, 'dp', pairs)  21.1 us
    all_gather x1, blocking collectives, on_device(): activated_all = lax.all_gather(activated, 'dp', axis=0, tiled=True)  20.7 us
    transpose x8, local copies, waits for them, and re-layouts, scattered_grad(): left_t = left.reshape(tokens, rows).T  14.3 us
  transfers between devices with their start and end apart: 50, of which 31 were waited for; matrix products, arithmetic and copies ran while one was open for 23% of the time, Pallas kernels for 0%

profile of v1, /device:TPU:0, one launch (start us, length us, event | category | flops | bytes accessed | tf_op | source)
XLA Modules:
  0.0 628.9 jit_solution(7763291434309436591)
XLA Ops:
  2.7 5.8 fusion.2
  26.7 15.8 %collective-permute-done.1 = f32[1,256,768]{2,1,0:T(8,128)S(1)} collective-permute-done((f32[1,256,768]{2,1,0:T(8,128)S(1)}, f32[1,256,768]{2,1,0:T(8,128)S(1)}, u32[]{:S(2)}, u32[]{:S(2)}) %collective-permute-start.1) | collective-permute-done | bytes 786464 | tf_op jit(solution)/shard_map/ppermute | solution.py:50
  48.9 5.5 fusion.77
  61.9 10.7 %collective-permute-done.2 = f32[1,256,768]{2,1,0:T(8,128)} collective-permute-done((f32[1,256,768]{2,1,0:T(8,128)S(1)}, f32[1,256,768]{2,1,0:T(8,128)}, u32[]{:S(2)}, u32[]{:S(2)}) %collective-permute-start.2) | collective-permute-done | bytes 786464 | tf_op jit(solution)/shard_map/ppermute | solution.py:50
  89.4 16.9 %collective-permute-done.3 = f32[1,256,768]{2,1,0:T(8,128)S(1)} collective-permute-done((f32[1,256,768]{2,1,0:T(8,128)S(1)}, f32[1,256,768]{2,1,0:T(8,128)S(1)}, u32[]{:S(2)}, u32[]{:S(2)}) %collective-permute-start.3) | collective-permute-done | bytes 786464 | tf_op jit(solution)/shard_map/ppermute | solution.py:50
  112.3 6.3 %fusion.212 = (f32[1536]{0:T(1024)}, f32[256,1536]{1,0:T(8,128)S(1)}) fusion(f32[256,1536]{1,0:T(8,128)S(1)} %fusion.43, f32[2,1536,768]{2,1,0:T(8,128)} %param.24, f32[1,256,768]{2,1,0:T(8,128)S(1)} %copy-done.60, f32[768]{0:T(1024)S(1)} %copy-done.143), kind=kOutput, calls=%fused_computation.408 | convolution fusion | flops 1819998720 | bytes 8659968 | tf_op jit(solution)/shard_map/bsd,fd->bsf/dot_general | solution.py:218
  121.6 5.0 fusion.83
  129.6 12.2 %collective-permute-done.5 = f32[1,256,768]{2,1,0:T(8,128)S(1)} collective-permute-done((f32[1,256,768]{2,1,0:T(8,128)S(1)}, f32[1,256,768]{2,1,0:T(8,128)S(1)}, u32[]{:S(2)}, u32[]{:S(2)}) %collective-permute-start.5) | collective-permute-done | bytes 786464 | tf_op jit(solution)/shard_map/ppermute | solution.py:50
  142.8 11.7 %collective-permute-done.4 = f32[1,256,768]{2,1,0:T(8,128)S(1)} collective-permute-done((f32[1,256,768]{2,1,0:T(8,128)S(1)}, f32[1,256,768]{2,1,0:T(8,128)S(1)}, u32[]{:S(2)}, u32[]{:S(2)}) %collective-permute-start.4) | collective-permute-done | bytes 786464 | tf_op jit(solution)/shard_map/ppermute | solution.py:50
  169.3 5.0 fusion.71
  174.6 20.7 %all-gather = f32[16,1,768]{2,1,0:T(1,128)S(1)} all-gather(f32[1,1,768]{2,1,0:T(1,128)S(1)} %copy-done.145), channel_id=1, replica_groups=mesh['dp'=16,'tensor'=2] {'dp'}, dimensions={0}, use_global_device_ids=true | all-gather | bytes 52224 | tf_op jit(solution)/shard_map/all_gather | solution.py:139
  215.5 5.9 fusion.213
  221.4 6.0 fusion.74
  249.6 6.2 collective-permute-done.25
  275.4 4.9 fusion.68
  314.4 5.7 fusion.3
  330.8 7.1 %collective-permute-done.27 = f32[4,48,384]{2,1,0:T(8,128)S(1)} collective-permute-done((f32[4,48,384]{2,1,0:T(8,128)S(1)}, f32[4,48,384]{2,1,0:T(8,128)S(1)}, u32[]{:S(2)}, u32[]{:S(2)}) %collective-permute-start.27) | collective-permute-done | bytes 294944 | tf_op jit(solution)/shard_map/ppermute | solution.py:106
  338.0 6.6 %collective-permute-done.31 = f32[4,48,384]{2,1,0:T(8,128)S(1)} collective-permute-done((f32[4,48,384]{2,1,0:T(8,128)S(1)}, f32[4,48,384]{2,1,0:T(8,128)S(1)}, u32[]{:S(2)}, u32[]{:S(2)}) %collective-permute-start.31) | collective-permute-done | bytes 294944 | tf_op jit(solution)/shard_map/ppermute | solution.py:106
  350.3 5.2 collective-permute-done.28
  355.8 5.6 collective-permute-done.32
  374.9 7.8 %collective-permute-done.21 = f32[8,6528]{1,0:T(8,128)S(1)} collective-permute-done((f32[8,6528]{1,0:T(8,128)S(1)}, f32[8,6528]{1,0:T(8,128)S(1)}, u32[]{:S(2)}, u32[]{:S(2)}) %collective-permute-start.21) | collective-permute-done | bytes 208928 | tf_op jit(solution)/shard_map/ppermute | solution.py:20
  423.3 9.0 %collective-permute-done.43 = f32[4,48,1536]{2,1,0:T(8,128)S(1)} collective-permute-done((f32[4,48,1536]{2,1,0:T(8,128)S(1)}, f32[4,48,1536]{2,1,0:T(8,128)S(1)}, u32[]{:S(2)}, u32[]{:S(2)}) %collective-permute-start.43) | collective-permute-done | bytes 1179680 | tf_op jit(solution)/shard_map/ppermute | solution.py:106
  434.0 23.6 %collective-permute-done.47 = f32[4,48,1536]{2,1,0:T(8,128)S(1)} collective-permute-done((f32[4,48,1536]{2,1,0:T(8,128)S(1)}, f32[4,48,1536]{2,1,0:T(8,128)S(1)}, u32[]{:S(2)}, u32[]{:S(2)}) %collective-permute-start.47) | collective-permute-done | bytes 1179680 | tf_op jit(solution)/shard_map/ppermute | solution.py:106
  457.8 13.3 %collective-permute-done.44 = f32[2,48,1536]{2,1,0:T(8,128)S(1)} collective-permute-done((f32[2,48,1536]{2,1,0:T(8,128)S(1)}, f32[2,48,1536]{2,1,0:T(8,128)S(1)}, u32[]{:S(2)}, u32[]{:S(2)}) %collective-permute-start.44) | collective-permute-done | bytes 589856 | tf_op jit(solution)/shard_map/ppermute | solution.py:106
  471.5 12.3 %collective-permute-done.48 = f32[2,48,1536]{2,1,0:T(8,128)S(1)} collective-permute-done((f32[2,48,1536]{2,1,0:T(8,128)S(1)}, f32[2,48,1536]{2,1,0:T(8,128)S(1)}, u32[]{:S(2)}, u32[]{:S(2)}) %collective-permute-start.48) | collective-permute-done | bytes 589856 | tf_op jit(solution)/shard_map/ppermute | solution.py:106
  484.2 43.0 %collective-permute-done.11 = f32[4,48,1152]{2,1,0:T(8,128)S(1)} collective-permute-done((f32[4,48,1152]{2,1,0:T(8,128)S(1)}, f32[4,48,1152]{2,1,0:T(8,128)S(1)}, u32[]{:S(2)}, u32[]{:S(2)}) %collective-permute-start.11) | collective-permute-done | bytes 884768 | tf_op jit(solution)/shard_map/ppermute | solution.py:106
  527.3 17.9 %collective-permute-done.15 = f32[4,48,1152]{2,1,0:T(8,128)S(1)} collective-permute-done((f32[4,48,1152]{2,1,0:T(8,128)S(1)}, f32[4,48,1152]{2,1,0:T(8,128)S(1)}, u32[]{:S(2)}, u32[]{:S(2)}) %collective-permute-start.15) | collective-permute-done | bytes 884768 | tf_op jit(solution)/shard_map/ppermute | solution.py:106
  550.9 7.3 %collective-permute-done.12 = f32[2,48,1152]{2,1,0:T(8,128)S(1)} collective-permute-done((f32[2,48,1152]{2,1,0:T(8,128)S(1)}, f32[2,48,1152]{2,1,0:T(8,128)S(1)}, u32[]{:S(2)}, u32[]{:S(2)}) %collective-permute-start.12) | collective-permute-done | bytes 442400 | tf_op jit(solution)/shard_map/ppermute | solution.py:106
  558.4 14.1 %collective-permute-done.16 = f32[2,48,1152]{2,1,0:T(8,128)S(1)} collective-permute-done((f32[2,48,1152]{2,1,0:T(8,128)S(1)}, f32[2,48,1152]{2,1,0:T(8,128)S(1)}, u32[]{:S(2)}, u32[]{:S(2)}) %collective-permute-start.16) | collective-permute-done | bytes 442400 | tf_op jit(solution)/shard_map/ppermute | solution.py:106
  572.6 22.6 %collective-permute-done.13 = f32[1,48,1152]{2,1,0:T(8,128)S(1)} collective-permute-done((f32[1,48,1152]{2,1,0:T(8,128)S(1)}, f32[1,48,1152]{2,1,0:T(8,128)S(1)}, u32[]{:S(2)}, u32[]{:S(2)}) %collective-permute-start.13) | collective-permute-done | bytes 221216 | tf_op jit(solution)/shard_map/ppermute | solution.py:106
  603.1 19.3 %collective-permute-done.37 = f32[1,48,1536]{2,1,0:T(8,128)S(1)} collective-permute-done((f32[1,48,1536]{2,1,0:T(8,128)S(1)}, f32[1,48,1536]{2,1,0:T(8,128)S(1)}, u32[]{:S(2)}, u32[]{:S(2)}) %collective-permute-start.37) | collective-permute-done | bytes 294944 | tf_op jit(solution)/shard_map/ppermute | solution.py:106
  622.5 5.1 collective-permute-done.41
  (645 shorter events, 261.3 us)
Async XLA Ops:
  23.4 19.1 %collective-permute-start.1 = (f32[1,256,768]{2,1,0:T(8,128)S(1)}, f32[1,256,768]{2,1,0:T(8,128)S(1)}, u32[]{:S(2)}, u32[]{:S(2)}) collective-permute-start(f32[1,256,768]{2,1,0:T(8,128)S(1)} %convolution_bitcast_fusion.3), channel_id=1, source_target_pairs={{0,1},{1,0},{2,3},{3,2},{4,5},{5,4},{6,7},{7,6},{8,9},{9,8},{10,11... | collective-permute-start | bytes 2359304 | tf_op jit(solution)/shard_map/ppermute | solution.py:50
  54.4 18.3 %collective-permute-start.2 = (f32[1,256,768]{2,1,0:T(8,128)S(1)}, f32[1,256,768]{2,1,0:T(8,128)}, u32[]{:S(2)}, u32[]{:S(2)}) collective-permute-start(f32[1,256,768]{2,1,0:T(8,128)S(1)} %fusion.77), channel_id=1, source_target_pairs={{0,1},{1,0},{2,3},{3,2},{4,5},{5,4},{6,7},{7,6},{8,9},{9,8},{10,11... | collective-permute-start | bytes 2359304 | tf_op jit(solution)/shard_map/ppermute | solution.py:50
  89.0 17.2 %collective-permute-start.3 = (f32[1,256,768]{2,1,0:T(8,128)S(1)}, f32[1,256,768]{2,1,0:T(8,128)S(1)}, u32[]{:S(2)}, u32[]{:S(2)}) collective-permute-start(f32[1,256,768]{2,1,0:T(8,128)S(1)} %convolution_bitcast_fusion.2), channel_id=1, source_target_pairs={{0,1},{1,0},{2,3},{3,2},{4,5},{5,4},{6,7},{7,6},{8,9},{9,8},{10,11... | collective-permute-start | bytes 2359304 | tf_op jit(solution)/shard_map/ppermute | solution.py:50
  121.3 20.5 %collective-permute-start.5 = (f32[1,256,768]{2,1,0:T(8,128)S(1)}, f32[1,256,768]{2,1,0:T(8,128)S(1)}, u32[]{:S(2)}, u32[]{:S(2)}) collective-permute-start(f32[1,256,768]{2,1,0:T(8,128)S(1)} %fusion.80), channel_id=1, source_target_pairs={{0,1},{1,0},{2,3},{3,2},{4,5},{5,4},{6,7},{7,6},{8,9},{9,8},{10,11... | collective-permute-start | bytes 2359304 | tf_op jit(solution)/shard_map/ppermute | solution.py:50
  126.6 27.8 %collective-permute-start.4 = (f32[1,256,768]{2,1,0:T(8,128)S(1)}, f32[1,256,768]{2,1,0:T(8,128)S(1)}, u32[]{:S(2)}, u32[]{:S(2)}) collective-permute-start(f32[1,256,768]{2,1,0:T(8,128)S(1)} %fusion.83), channel_id=1, source_target_pairs={{0,1},{1,0},{2,3},{3,2},{4,5},{5,4},{6,7},{7,6},{8,9},{9,8},{10,11... | collective-permute-start | bytes 2359304 | tf_op jit(solution)/shard_map/ppermute | solution.py:50
  174.3 31.3 %collective-permute-start.6 = (f32[1,256,768]{2,1,0:T(8,128)}, f32[1,256,768]{2,1,0:T(8,128)}, u32[]{:S(2)}, u32[]{:S(2)}) collective-permute-start(f32[1,256,768]{2,1,0:T(8,128)} %fusion.71), channel_id=1, source_target_pairs={{0,1},{1,0},{2,3},{3,2},{4,5},{5,4},{6,7},{7,6},{8,9},{9,8},{10,11... | collective-permute-start | bytes 2359304 | tf_op jit(solution)/shard_map/ppermute | solution.py:50
  215.5 16.0 %collective-permute-start.22 = (f32[1,6528]{1,0:T(1,128)}, f32[1,6528]{1,0:T(1,128)}, u32[]{:S(2)}, u32[]{:S(2)}) collective-permute-start(f32[1,6528]{1,0:T(1,128)} %pad_maximum_fusion.14), channel_id=1, source_target_pairs={{0,30},{2,0},{4,2},{6,4},{8,6},{10,8},{12,10},{14,12},{16,14},{18,... | collective-permute-start | bytes 78344 | tf_op jit(solution)/shard_map/ppermute | solution.py:20
  227.4 31.9 %collective-permute-start.7 = (f32[1,256,768]{2,1,0:T(8,128)}, f32[1,256,768]{2,1,0:T(8,128)}, u32[]{:S(2)}, u32[]{:S(2)}) collective-permute-start(f32[1,256,768]{2,1,0:T(8,128)} %fusion.74), channel_id=1, source_target_pairs={{0,1},{1,0},{2,3},{3,2},{4,5},{5,4},{6,7},{7,6},{8,9},{9,8},{10,11... | collective-permute-start | bytes 2359304 | tf_op jit(solution)/shard_map/ppermute | solution.py:50
  240.5 159.1 %collective-permute-start.42 = (f32[384,1536]{1,0:T(8,128)}, f32[384,1536]{1,0:T(8,128)}, u32[]{:S(2)}, u32[]{:S(2)}) collective-permute-start(f32[384,1536]{1,0:T(8,128)} %fusion.188), channel_id=1, source_target_pairs={{0,2},{2,0},{4,6},{6,4},{8,10},{10,8},{12,14},{14,12},{16,18},{18,... | collective-permute-start | bytes 7077896 | tf_op jit(solution)/shard_map/ppermute | solution.py:96
  248.2 155.3 %collective-permute-start.46 = (f32[384,1536]{1,0:T(8,128)}, f32[384,1536]{1,0:T(8,128)}, u32[]{:S(2)}, u32[]{:S(2)}) collective-permute-start(f32[384,1536]{1,0:T(8,128)} %fusion.189), channel_id=1, source_target_pairs={{0,2},{2,0},{4,6},{6,4},{8,10},{10,8},{12,14},{14,12},{16,18},{18,... | collective-permute-start | bytes 7077896 | tf_op jit(solution)/shard_map/ppermute | solution.py:96
  280.3 18.8 %collective-permute-start.8 = (f32[1,256,768]{2,1,0:T(8,128)}, f32[1,256,768]{2,1,0:T(8,128)}, u32[]{:S(2)}, u32[]{:S(2)}) collective-permute-start(f32[1,256,768]{2,1,0:T(8,128)} %fusion.68), channel_id=1, source_target_pairs={{0,1},{1,0},{2,3},{3,2},{4,5},{5,4},{6,7},{7,6},{8,9},{9,8},{10,11... | collective-permute-start | bytes 2359304 | tf_op jit(solution)/shard_map/ppermute | solution.py:50
  292.0 116.3 %collective-permute-start.34 = (f32[384,1536]{1,0:T(8,128)}, f32[384,1536]{1,0:T(8,128)}, u32[]{:S(2)}, u32[]{:S(2)}) collective-permute-start(f32[384,1536]{1,0:T(8,128)} %fusion.220), channel_id=1, source_target_pairs={{0,2},{2,0},{4,6},{6,4},{8,10},{10,8},{12,14},{14,12},{16,18},{18,... | collective-permute-start | bytes 7077896 | tf_op jit(solution)/shard_map/ppermute | solution.py:96
  292.6 120.1 %collective-permute-start.38 = (f32[384,1536]{1,0:T(8,128)}, f32[384,1536]{1,0:T(8,128)}, u32[]{:S(2)}, u32[]{:S(2)}) collective-permute-start(f32[384,1536]{1,0:T(8,128)} %fusion.221), channel_id=1, source_target_pairs={{0,2},{2,0},{4,6},{6,4},{8,10},{10,8},{12,14},{14,12},{16,18},{18,... | collective-permute-start | bytes 7077896 | tf_op jit(solution)/shard_map/ppermute | solution.py:96
  304.2 18.2 %collective-permute-start.18 = (f32[1,6528]{1,0:T(1,128)S(1)}, f32[1,6528]{1,0:T(1,128)S(1)}, u32[]{:S(2)}, u32[]{:S(2)}) collective-permute-start(f32[1,6528]{1,0:T(1,128)S(1)} %pad_maximum_fusion.13), channel_id=1, source_target_pairs={{0,30},{2,0},{4,2},{6,4},{8,6},{10,8},{12,10},{14,12},{16,14},{18,... | collective-permute-start | bytes 78344 | tf_op jit(solution)/shard_map/ppermute | solution.py:20
  382.7 34.3 %collective-permute-start.10 = (f32[384,1152]{1,0:T(8,128)}, f32[384,1152]{1,0:T(8,128)}, u32[]{:S(2)}, u32[]{:S(2)}) collective-permute-start(f32[384,1152]{1,0:T(8,128)} %fusion.216), channel_id=1, source_target_pairs={{0,2},{2,0},{4,6},{6,4},{8,10},{10,8},{12,14},{14,12},{16,18},{18,... | collective-permute-start | bytes 5308424 | tf_op jit(solution)/shard_map/ppermute | solution.py:96
  399.6 21.3 %collective-permute-start.14 = (f32[384,1152]{1,0:T(8,128)}, f32[384,1152]{1,0:T(8,128)S(1)}, u32[]{:S(2)}, u32[]{:S(2)}) collective-permute-start(f32[384,1152]{1,0:T(8,128)} %fusion.217), channel_id=1, source_target_pairs={{0,2},{2,0},{4,6},{6,4},{8,10},{10,8},{12,14},{14,12},{16,18},{18,... | collective-permute-start | bytes 5308424 | tf_op jit(solution)/shard_map/ppermute | solution.py:96
  403.4 28.9 %collective-permute-start.43 = (f32[4,48,1536]{2,1,0:T(8,128)S(1)}, f32[4,48,1536]{2,1,0:T(8,128)S(1)}, u32[]{:S(2)}, u32[]{:S(2)}) collective-permute-start(f32[4,48,1536]{2,1,0:T(8,128)S(1)} %dynamic-slice_bitcast_fusion.1), channel_id=1, source_target_pairs={{0,4},{2,6},{4,0},{6,2},{8,12},{10,14},{12,8},{14,10},{16,20},{18,... | collective-permute-start | bytes 3538952 | tf_op jit(solution)/shard_map/ppermute | solution.py:106
  408.3 49.3 %collective-permute-start.47 = (f32[4,48,1536]{2,1,0:T(8,128)S(1)}, f32[4,48,1536]{2,1,0:T(8,128)S(1)}, u32[]{:S(2)}, u32[]{:S(2)}) collective-permute-start(f32[4,48,1536]{2,1,0:T(8,128)S(1)} %dynamic-slice_bitcast_fusion), channel_id=1, source_target_pairs={{0,4},{2,6},{4,0},{6,2},{8,12},{10,14},{12,8},{14,10},{16,20},{18,... | collective-permute-start | bytes 3538952 | tf_op jit(solution)/shard_map/ppermute | solution.py:106
  412.7 132.6 %collective-permute-start.35 = (f32[4,48,1536]{2,1,0:T(8,128)S(1)}, f32[4,48,1536]{2,1,0:T(8,128)S(1)}, u32[]{:S(2)}, u32[]{:S(2)}) collective-permute-start(f32[4,48,1536]{2,1,0:T(8,128)S(1)} %dynamic-slice_bitcast_fusion.3), channel_id=1, source_target_pairs={{0,4},{2,6},{4,0},{6,2},{8,12},{10,14},{12,8},{14,10},{16,20},{18,... | collective-permute-start | bytes 3538952 | tf_op jit(solution)/shard_map/ppermute | solution.py:106
  417.1 130.6 %collective-permute-start.39 = (f32[4,48,1536]{2,1,0:T(8,128)S(1)}, f32[4,48,1536]{2,1,0:T(8,128)S(1)}, u32[]{:S(2)}, u32[]{:S(2)}) collective-permute-start(f32[4,48,1536]{2,1,0:T(8,128)S(1)} %dynamic-slice_bitcast_fusion.2), channel_id=1, source_target_pairs={{0,4},{2,6},{4,0},{6,2},{8,12},{10,14},{12,8},{14,10},{16,20},{18,... | collective-permute-start | bytes 3538952 | tf_op jit(solution)/shard_map/ppermute | solution.py:106
  421.0 106.2 %collective-permute-start.11 = (f32[4,48,1152]{2,1,0:T(8,128)S(1)}, f32[4,48,1152]{2,1,0:T(8,128)S(1)}, u32[]{:S(2)}, u32[]{:S(2)}) collective-permute-start(f32[4,48,1152]{2,1,0:T(8,128)S(1)} %dynamic-slice_bitcast_fusion.5), channel_id=1, source_target_pairs={{0,4},{2,6},{4,0},{6,2},{8,12},{10,14},{12,8},{14,10},{16,20},{18,... | collective-permute-start | bytes 2654216 | tf_op jit(solution)/shard_map/ppermute | solution.py:106
  432.3 112.8 %collective-permute-start.15 = (f32[4,48,1152]{2,1,0:T(8,128)S(1)}, f32[4,48,1152]{2,1,0:T(8,128)S(1)}, u32[]{:S(2)}, u32[]{:S(2)}) collective-permute-start(f32[4,48,1152]{2,1,0:T(8,128)S(1)} %dynamic-slice_bitcast_fusion.4), channel_id=1, source_target_pairs={{0,4},{2,6},{4,0},{6,2},{8,12},{10,14},{12,8},{14,10},{16,20},{18,... | collective-permute-start | bytes 2654216 | tf_op jit(solution)/shard_map/ppermute | solution.py:106
  457.6 13.5 %collective-permute-start.44 = (f32[2,48,1536]{2,1,0:T(8,128)S(1)}, f32[2,48,1536]{2,1,0:T(8,128)S(1)}, u32[]{:S(2)}, u32[]{:S(2)}) collective-permute-start(f32[2,48,1536]{2,1,0:T(8,128)S(1)} %dynamic-slice_bitcast_fusion.7), channel_id=1, source_target_pairs={{0,8},{2,10},{4,12},{6,14},{8,0},{10,2},{12,4},{14,6},{16,24},{18,... | collective-permute-start | bytes 1769480 | tf_op jit(solution)/shard_map/ppermute | solution.py:106
  483.7 64.2 %collective-permute-start.45 = (f32[1,48,1536]{2,1,0:T(8,128)S(1)}, f32[1,48,1536]{2,1,0:T(8,128)S(1)}, u32[]{:S(2)}, u32[]{:S(2)}) collective-permute-start(f32[1,48,1536]{2,1,0:T(8,128)S(1)} %constant_dynamic-slice_fusion.4), channel_id=1, source_target_pairs={{0,16},{2,18},{4,20},{6,22},{8,24},{10,26},{12,28},{14,30},{16,0},... | collective-permute-start | bytes 884744 | tf_op jit(solution)/shard_map/ppermute | solution.py:106
  527.1 22.9 %collective-permute-start.49 = (f32[1,48,1536]{2,1,0:T(8,128)S(1)}, f32[1,48,1536]{2,1,0:T(8,128)S(1)}, u32[]{:S(2)}, u32[]{:S(2)}) collective-permute-start(f32[1,48,1536]{2,1,0:T(8,128)S(1)} %constant_dynamic-slice_fusion.1), channel_id=1, source_target_pairs={{0,16},{2,18},{4,20},{6,22},{8,24},{10,26},{12,28},{14,30},{16,0},... | collective-permute-start | bytes 884744 | tf_op jit(solution)/shard_map/ppermute | solution.py:106
  545.3 27.2 %collective-permute-start.16 = (f32[2,48,1152]{2,1,0:T(8,128)S(1)}, f32[2,48,1152]{2,1,0:T(8,128)S(1)}, u32[]{:S(2)}, u32[]{:S(2)}) collective-permute-start(f32[2,48,1152]{2,1,0:T(8,128)S(1)} %dynamic-slice_bitcast_fusion.10), channel_id=1, source_target_pairs={{0,8},{2,10},{4,12},{6,14},{8,0},{10,2},{12,4},{14,6},{16,24},{18,... | collective-permute-start | bytes 1327112 | tf_op jit(solution)/shard_map/ppermute | solution.py:106
  547.6 51.7 %collective-permute-start.36 = (f32[2,48,1536]{2,1,0:T(8,128)S(1)}, f32[2,48,1536]{2,1,0:T(8,128)S(1)}, u32[]{:S(2)}, u32[]{:S(2)}) collective-permute-start(f32[2,48,1536]{2,1,0:T(8,128)S(1)} %dynamic-slice_bitcast_fusion.9), channel_id=1, source_target_pairs={{0,8},{2,10},{4,12},{6,14},{8,0},{10,2},{12,4},{14,6},{16,24},{18,... | collective-permute-start | bytes 1769480 | tf_op jit(solution)/shard_map/ppermute | solution.py:106
  547.9 55.0 %collective-permute-start.40 = (f32[2,48,1536]{2,1,0:T(8,128)S(1)}, f32[2,48,1536]{2,1,0:T(8,128)S(1)}, u32[]{:S(2)}, u32[]{:S(2)}) collective-permute-start(f32[2,48,1536]{2,1,0:T(8,128)S(1)} %dynamic-slice_bitcast_fusion.8), channel_id=1, source_target_pairs={{0,8},{2,10},{4,12},{6,14},{8,0},{10,2},{12,4},{14,6},{16,24},{18,... | collective-permute-start | bytes 1769480 | tf_op jit(solution)/shard_map/ppermute | solution.py:106
  558.3 36.9 %collective-permute-start.13 = (f32[1,48,1152]{2,1,0:T(8,128)S(1)}, f32[1,48,1152]{2,1,0:T(8,128)S(1)}, u32[]{:S(2)}, u32[]{:S(2)}) collective-permute-start(f32[1,48,1152]{2,1,0:T(8,128)S(1)} %constant_dynamic-slice_fusion.22), channel_id=1, source_target_pairs={{0,16},{2,18},{4,20},{6,22},{8,24},{10,26},{12,28},{14,30},{16,0},... | collective-permute-start | bytes 663560 | tf_op jit(solution)/shard_map/ppermute | solution.py:106
  572.6 25.9 %collective-permute-start.17 = (f32[1,48,1152]{2,1,0:T(8,128)S(1)}, f32[1,48,1152]{2,1,0:T(8,128)S(1)}, u32[]{:S(2)}, u32[]{:S(2)}) collective-permute-start(f32[1,48,1152]{2,1,0:T(8,128)S(1)} %constant_dynamic-slice_fusion.19), channel_id=1, source_target_pairs={{0,16},{2,18},{4,20},{6,22},{8,24},{10,26},{12,28},{14,30},{16,0},... | collective-permute-start | bytes 663560 | tf_op jit(solution)/shard_map/ppermute | solution.py:106
  599.4 23.0 %collective-permute-start.37 = (f32[1,48,1536]{2,1,0:T(8,128)S(1)}, f32[1,48,1536]{2,1,0:T(8,128)S(1)}, u32[]{:S(2)}, u32[]{:S(2)}) collective-permute-start(f32[1,48,1536]{2,1,0:T(8,128)S(1)} %constant_dynamic-slice_fusion.10), channel_id=1, source_target_pairs={{0,16},{2,18},{4,20},{6,22},{8,24},{10,26},{12,28},{14,30},{16,0},... | collective-permute-start | bytes 884744 | tf_op jit(solution)/shard_map/ppermute | solution.py:106
  603.0 24.5 %collective-permute-start.41 = (f32[1,48,1536]{2,1,0:T(8,128)S(1)}, f32[1,48,1536]{2,1,0:T(8,128)S(1)}, u32[]{:S(2)}, u32[]{:S(2)}) collective-permute-start(f32[1,48,1536]{2,1,0:T(8,128)S(1)} %constant_dynamic-slice_fusion.7), channel_id=1, source_target_pairs={{0,16},{2,18},{4,20},{6,22},{8,24},{10,26},{12,28},{14,30},{16,0},... | collective-permute-start | bytes 884744 | tf_op jit(solution)/shard_map/ppermute | solution.py:106
  (178 other events, 1185.3 us)
